TPU v7x, 32 devices: a whole 2x2x4 slice. The times are simulated.
32 devices in a mesh: grp: 2 (over x), row: 8 (over z, y), col: 2 (over core).
Axes of the slice: x: 2, y: 2, z: 4, core: 2. Of those that a mesh axis runs over, the one named last changes fastest.
Arguments:
- pair_act: bfloat16 [64, 32, 128], P(('grp', 'row'), 'col'), parts along dimension 0, may hold values from -200 to 200
- cotangent: bfloat16 [64, 32, 128], P(('grp', 'row'), 'col'), parts along dimension 0, may hold values from -6 to 6
- residue_mask: int32 [64], P('grp'), parts along dimension 0, may hold values from 0 to 1, as said below
- front_weight: bfloat16 [2, 128, 640], replicated, may hold values from -0.5 to 0.5
- out_weight: bfloat16 [2, 128, 128], replicated, may hold values from -0.5 to 0.5
Outputs:
- pair_grad: bfloat16 [64, 32, 128], P(('grp', 'row'), 'col'), parts along dimension 0
There are 2 independent parts, one for each index of `grp`. A program takes and returns all parts, laid end to end along the dimension named above; an argument that names none is the same for every part. Nothing has to cross between parts.
Inputs may be any that keep to these rules, and one draw needn't show every extreme that they name: residue_mask is 1 on residues 0 to L - 1 and 0 from L on, for a chain length L of at least 24.
All inputs are finite; a program needn't handle non-finite values.
Results may differ from a plain program's by a relative error of at most 0.01.
Values may be sent and summed in bfloat16 or wider, within the bound.
A program may use at most 64 MiB of HBM per device.

v0:
```python
import functools

import jax
import jax.numpy as jnp
from jax import lax
from jax.experimental import pallas as pl
from jax.experimental.pallas import tpu as pltpu
from jax.sharding import PartitionSpec as P

H = 128
TILE = 8
F32 = jnp.float32
BF16 = jnp.bfloat16
MESH = pl.DeviceIdType.MESH
VMEM_BUDGET = 24 << 20
FULL_ARRAYS = 16


def sigmoid(x):
    return 0.5 * jnp.tanh(0.5 * x) + 0.5


def norm(v):
    centred = v - jnp.mean(v, axis=-1, keepdims=True)
    r = lax.rsqrt(jnp.mean(centred * centred, axis=-1, keepdims=True) + 1e-05)
    return centred * r, r


def scales(v):
    mean = jnp.mean(v, axis=-1, keepdims=True)
    centred = v - mean
    r = lax.rsqrt(jnp.mean(centred * centred, axis=-1, keepdims=True) + 1e-05)
    return r, r * mean


def column_sums(w):
    return jnp.sum(w.astype(F32), axis=0, keepdims=True)


def norm_back(y, r, d):
    return r * (d - jnp.mean(d, axis=-1, keepdims=True) - y * jnp.mean(d * y, axis=-1, keepdims=True))


def rounded(v):
    return v.astype(BF16).astype(F32)


def dot(a, b):
    return jnp.dot(a.astype(BF16), b, preferred_element_type=F32)


def dot_t(a, b):
    return lax.dot_general(
        a.astype(BF16), b, (((1,), (1,)), ((), ())), preferred_element_type=F32
    )


def part(p, n):
    return p[:, n * H : (n + 1) * H]


def factors(x, mask, weight):
    y, r = norm(x)
    p = dot(y, weight)
    s0, s2, s4 = sigmoid(part(p, 0)), sigmoid(part(p, 2)), sigmoid(part(p, 4))
    fa, fb = mask * s0, mask * s2
    return y, r, fa * part(p, 1) * (1.0 - s0), fa, fb * part(p, 3) * (1.0 - s2), fb, s4 * (1.0 - s4)


def front_back(f, weight, d_a, d_b, d_gate):
    y, r, f0, f1, f2, f3, f4 = f
    d = jnp.concatenate(
        [(v.astype(BF16)) for v in (d_a * f0, d_a * f1, d_b * f2, d_b * f3, d_gate * f4)], axis=1
    )
    return rounded(norm_back(y, r, rounded(dot_t(d, weight))))


def crop_kernel(
    rows, pair, cot, mask_in, wf_in, wo_in, out,
    x_h, ct_h, x_far, wf, wo, chain,
    left, right, in_left, in_right, sig, left_t, right_t, flip_r, flip_s,
    mask, mixed, gate, mid, in_mixed, in_gate, ct32, normed, along,
    saved, d_left, d_right, sig_row, sig_col, sig_out, sig_got,
    local_sem, x_send, x_recv, ct_send, ct_recv, psend, precv, ready, far_send, far_recv,
):
    n, c = left.shape[0], left.shape[2]
    lr, lc = out.shape[0], out.shape[1]
    bits = rows.bit_length() - 1
    me, my_col = lax.axis_index("row"), lax.axis_index("col")
    other = 1 - my_col
    me_bits = [lax.rem(lax.div(me, 1 << b), 2) for b in range(bits)]

    def flip(d, low=0):
        total = 0
        for b in range(low, bits):
            bit = me_bits[b]
            total = total + (1 - bit if d >> b & 1 else bit) * (1 << b)
        return total

    far = rows - 2 if rows > 4 else rows
    wide_row = jnp.logical_and(me >= far, my_col == 0)
    near_row = jnp.logical_and(me == 0, rows > 4)
    barrier = pltpu.get_barrier_semaphore()
    pl.semaphore_signal(barrier, inc=1, device_id={"col": other}, device_id_type=MESH)
    for row in range(1, rows):
        @pl.when(jnp.logical_and(me < row, me != row - 1) if row == far else me < row)
        def _():
            pl.semaphore_signal(barrier, inc=1, device_id={"row": row}, device_id_type=MESH)

    for row in range(far, rows):
        @pl.when(jnp.logical_and(me == 0, my_col == 1))
        def _():
            pl.semaphore_signal(
                barrier, inc=1, device_id={"row": row, "col": 0}, device_id_type=MESH
            )

    r0 = pl.multiple_of(me * lr, lr)
    c0 = pl.multiple_of(my_col * lc, lc)
    o0 = pl.multiple_of(other * lc, lc)
    jl = lax.rem(me * lr, lc)
    owner = lax.div(me * lr, lc) == my_col

    own = [
        pltpu.make_async_copy(src, dst.at[pl.ds(r0, lr)], local_sem.at[t])
        for t, (src, dst) in enumerate(((pair, x_h), (cot, ct_h)))
    ]
    weights = [
        pltpu.make_async_copy(wf_in, wf, local_sem.at[2]),
        pltpu.make_async_copy(wo_in, wo, local_sem.at[3]),
    ]
    chain_copy = pltpu.make_async_copy(mask_in, chain, local_sem.at[4])
    for copy in [chain_copy, own[0]] + weights + [own[1]]:
        copy.start()

    def direct(t, row, mine=None):
        src, dst = ((pair, x_h), (cot, ct_h))[t]
        source = row if mine is None else mine
        return pltpu.make_async_remote_copy(
            src_ref=src,
            dst_ref=dst.at[pl.ds(pl.multiple_of(source * lr, lr), lr)],
            send_sem=x_send.at[row] if t == 0 else ct_send.at[0],
            recv_sem=x_recv.at[source] if t == 0 else ct_recv.at[0],
            device_id={"row": row},
            device_id_type=MESH,
        )

    def lower(step, start=0):
        for row in range(start, rows - 1):
            @pl.when(jnp.logical_and(row < me, me != far) if row == far - 1 else row < me)
            def _():
                step(row)

    def higher(step):
        for row in range(1, rows):
            @pl.when(jnp.logical_or(row > me, me == far) if row == far - 1 else row > me)
            def _():
                step(row)

    def far_copy():
        at = pl.ds(pl.multiple_of((me - far) * lr, lr), lr)
        return pltpu.make_async_remote_copy(
            src_ref=pair,
            dst_ref=x_far.at[at],
            send_sem=far_send.at[0],
            recv_sem=far_recv.at[me - far],
            device_id={"row": 0, "col": 1},
            device_id_type=MESH,
        )

    def answer(row):
        if row == 0:
            @pl.when(jnp.logical_not(wide_row))
            def _():
                direct(0, row, me).start()
        elif row < 2:
            direct(0, row, me).start()
        pl.semaphore_signal(ready.at[me], inc=1, device_id={"row": row}, device_id_type=MESH)

    def send(row):
        if row >= 2:
            direct(0, row, me).start()

    def tell(row, about):
        pl.semaphore_signal(ready.at[about], inc=1, device_id={"row": row}, device_id_type=MESH)

    def follow(row):
        pl.semaphore_wait(ready.at[row], 1)
        direct(0, row, me).start()
        if row == far:
            @pl.when(me == far - 2)
            def _():
                tell(far, far - 1)
                tell(far - 1, far)

    def drain(row):
        direct(0, row, me).wait_send()

    def second(row):
        direct(1, row, me).start()

    def partner(q, r, ref):
        return pltpu.make_async_remote_copy(
            src_ref=ref,
            dst_ref=ref,
            send_sem=psend.at[q],
            recv_sem=precv.at[r],
            device_id={"col": other},
            device_id_type=MESH,
        )

    greeted = me + 1 - jnp.where(me == far, 1, 0)
    pl.semaphore_wait(barrier, greeted + jnp.where(wide_row, 1, 0))

    @pl.when(wide_row)
    def _():
        direct(0, 0, me).start()
        far_copy().start()

    lower(answer)

    chain_copy.wait()
    span = jnp.broadcast_to(chain[...].astype(F32), (n, n))
    here = lax.broadcasted_iota(jnp.int32, (n, n), 0) == lax.broadcasted_iota(jnp.int32, (n, n), 1)
    along[...] = jnp.broadcast_to(
        jnp.sum(jnp.where(here, span, 0.0), axis=1, keepdims=True), (n, c)
    )
    across = along[pl.ds(c0, lc), :]
    for i in range(n):
        mask[i * lc : (i + 1) * lc] = across * along[i : i + 1]
    lower(send)

    def block(ref, k0, nk):
        return ref[pl.ds(pl.multiple_of(k0 * lc, lc), nk * lc), :]

    def put(ref, k0, nk, v):
        ref[pl.ds(pl.multiple_of(k0 * lc, lc), nk * lc), :] = v

    def put_half(ref, k0, nk, v):
        ref[pl.ds(k0, nk), pl.ds(c0, lc), :] = v.reshape(nk, lc, c)

    def half(ref, k0, nk):
        return ref.at[pl.ds(k0, nk), pl.ds(c0, lc)]

    def projected(x, segments, weight, sums, a_ref, b_ref, g_ref):
        r, rm = scales(x.astype(F32))
        p = dot(x, weight)

        def part(p, q):
            return p[:, q * H : (q + 1) * H] * r - rm * sums[:, q * H : (q + 1) * H]

        m = jnp.concatenate([block(mask, k0, nk) for k0, nk in segments], axis=0)
        a = rounded(sigmoid(part(p, 0)) * part(p, 1) * m)
        b = rounded(sigmoid(part(p, 2)) * part(p, 3) * m)
        g = sigmoid(part(p, 4))
        at = 0
        for k0, nk in segments:
            span = slice(at * lc, (at + nk) * lc)
            put_half(a_ref, k0, nk, a[span])
            put_half(b_ref, k0, nk, b[span])
            put(g_ref, k0, nk, g[span])
            at += nk

    def triangle(count, width, first, depth, row_at, tile_at, acc=None):
        def term(q, acc):
            t = tile_at(first + q)
            return tuple(v + row_at(a, first + q) * t for a, v in enumerate(acc))

        if acc is None:
            acc = (jnp.zeros((width, c), F32),) * count
        return lax.fori_loop(0, depth, term, tuple(acc), unroll=True)

    def loop(count, step):
        def body(k, carry):
            step(k)
            return carry

        lax.fori_loop(0, count, body, 0)

    for copy in weights:
        copy.wait()
    sums_out, sums_in, sums_mix = (column_sums(w) for w in (wf[0], wf[1], wo[0]))
    groups = [[(0, 1)], [(1, 1), (2, 2)] if rows > 2 else [(1, 1)]]
    groups += [[(d, 2)] for d in range(4, rows, 2)]
    for g, group in enumerate(groups):
        for d, count in group:
            for q in range(d, d + count):
                if q == 0:
                    own[0].wait()
                else:
                    direct(0, flip(q)).wait_recv()
        segments = [
            (pl.multiple_of(flip(d, count.bit_length() - 1) * lr, count * lr), count * lr)
            for d, count in group
        ]
        x = jnp.concatenate(
            [x_h[pl.ds(k0, nk)].reshape(nk * lc, c) for k0, nk in segments], axis=0
        )
        projected(x, segments, wf[0], sums_out, left, right, gate)
        def exchange():
            for k0, nk in segments:
                partner(0, 0, half(left, k0, nk)).start()
                partner(0, 0, half(right, k0, nk)).start()

        if g == len(groups) - 1 and rows > 4:
            pl.when(jnp.logical_not(jnp.logical_and(near_row, my_col == 0)))(exchange)
        else:
            exchange()
        if g == 0:
            higher(follow)

            @pl.when(me > 0)
            def _():
                second(0)

            lower(drain)
            pl.semaphore_signal(
                ready.at[rows], inc=1, device_id={"col": other}, device_id_type=MESH
            )
            pl.semaphore_wait(ready.at[rows], 1)
            lower(second, 1)
        if g == len(groups) - 1:
            higher(second)

    group = TILE

    def outgoing(k0, fresh):
        for b in range(lc // TILE):
            t = jnp.swapaxes(right[pl.ds(c0 + b * TILE, TILE), pl.ds(k0, lc), :], 0, 1)
            flip_r[:, b * TILE : (b + 1) * TILE, :] = t

        def step(b):
            i0 = b * group
            base = pl.multiple_of(i0 * lc, lc * group)
            acc = None
            if not fresh:
                acc = [mixed[pl.ds(base + a * lc, lc), :] for a in range(group)]
            acc = triangle(
                group, lc, 0, lc,
                lambda a, q: left[i0 + a, pl.ds(k0 + q, 1), :],
                lambda q: flip_r[q],
                acc,
            )
            for a in range(group):
                mixed[pl.ds(base + a * lc, lc), :] = acc[a]

        loop(n // group, step)

    outgoing(c0, True)

    @pl.when(jnp.logical_and(near_row, my_col == 1))
    def _():
        for q in range(2):
            pltpu.make_async_remote_copy(
                src_ref=pair,
                dst_ref=x_far.at[pl.ds(q * lr, lr)],
                send_sem=far_send.at[0],
                recv_sem=far_recv.at[q],
                device_id={"row": 0, "col": 0},
                device_id_type=MESH,
            ).wait_recv()
        x = x_far[...].reshape(2 * lr * lc, c)
        r, rm = scales(x.astype(F32))
        p = dot(x, wf[0, :, : 4 * H])

        def scaled(q):
            return part(p, q) * r - rm * part(sums_out, q)

        k0 = far * lr
        over = along[pl.ds(o0, lc), :]
        m = jnp.concatenate([over * along[k0 + i : k0 + i + 1] for i in range(2 * lr)], axis=0)
        a = rounded(sigmoid(scaled(0)) * scaled(1) * m)
        b = rounded(sigmoid(scaled(2)) * scaled(3) * m)
        left[k0:, pl.ds(o0, lc), :] = a.reshape(2 * lr, lc, c)
        right[k0:, pl.ds(o0, lc), :] = b.reshape(2 * lr, lc, c)

    def pair_bytes(column, step):
        @pl.when(jnp.logical_and(near_row, my_col == column))
        def _():
            step(partner(0, 0, left.at[pl.ds(0, far * lr)]))

        @pl.when(jnp.logical_not(jnp.logical_and(near_row, my_col == column)))
        def _():
            step(partner(0, 0, left))

    pair_bytes(1, lambda copy: copy.wait_recv())
    outgoing(o0, False)

    v = mixed[...]
    r, rm = scales(v)
    high = v.astype(BF16)
    low = (v - high.astype(F32)).astype(BF16)
    update = dot(
        jnp.concatenate([high, low], axis=1), jnp.concatenate([wo[0], wo[0]], axis=0)
    )
    x = x_h[...].reshape(n * lc, c).astype(F32)
    x = rounded(x + gate[...] * (update * r - rm * sums_mix))
    mid[...] = x
    r, rm = scales(x)

    def scaled(p, q, at):
        return part(p, q) * r - rm * part(sums_in, at + q)

    x = x.astype(BF16)
    normed[...] = x
    p = dot(x, wf[1, :, : 2 * H])
    put_half(in_left, 0, n, rounded(sigmoid(scaled(p, 0, 0)) * scaled(p, 1, 0) * mask[...]))
    e_in_left = [
        partner(1, 1 + b, in_left.at[:, pl.ds(c0 + b * TILE, TILE)]) for b in range(lc // TILE)
    ]
    for copy in e_in_left:
        copy.start()
    p = dot(normed[...], wf[1, :, 2 * H :])
    v = rounded(sigmoid(scaled(p, 0, 2)) * scaled(p, 1, 2) * mask[...])
    put_half(in_right, 0, n, v)
    in_gate[...] = sigmoid(scaled(p, 2, 2))
    e_in_right = partner(1, 3, half(in_right, 0, n))
    e_in_right.start()

    def incoming(i0, copies=()):
        few = 4

        def step(i1):
            acc = triangle(
                few, lc, 0, n,
                lambda a, q: in_left[q, pl.ds(i1 + a, 1), :],
                lambda q: in_right[q, pl.ds(c0, lc), :],
            )
            for a in range(few):
                in_mixed[pl.ds(pl.multiple_of((i1 + a) * lc, lc), lc), :] = acc[a]

        for b in range(lc // TILE):
            if copies:
                copies[b].wait_recv()
            for a in range(0, TILE, few):
                step(pl.multiple_of(i0 + b * TILE, TILE) + a)

    nr, nc = lr * lc, lr * n

    def row_of(ref):
        return ref[pl.ds(pl.multiple_of(r0 * lc, lc), nr), :]

    def col_of(ref):
        return jnp.concatenate([ref[pl.ds(jl + a, n, stride=lc), :] for a in range(lr)], axis=0)

    def strips(ref, wide):
        return jnp.concatenate([row_of(ref), col_of(ref)], axis=0) if wide else row_of(ref)

    def each(step, here=True):
        @pl.when(jnp.logical_and(here, owner))
        def _():
            step(True, nr + nc)

        @pl.when(jnp.logical_and(here, jnp.logical_not(owner)))
        def _():
            step(False, nr)

    def transposed(src, dst, j0):
        for b in range(n // TILE):
            t = jnp.swapaxes(src[b * TILE : (b + 1) * TILE, pl.ds(j0, lc), :], 0, 1)
            dst[pl.ds(j0, lc), b * TILE : (b + 1) * TILE, :] = t

    incoming(c0)

    def prepare(wide, m):
        f = factors(strips(mid, wide), strips(mask, wide), wf[1])
        for q, v in enumerate(f):
            saved[q, :m] = jnp.broadcast_to(v, (m, c))

    def early(wide, m):
        prepare(wide, m)
        if wide:
            transposed(in_left, left_t, c0)
            transposed(in_right, right_t, c0)

    each(early, my_col == 0)

    incoming(o0, e_in_left)

    others = pl.ds(0, (rows - 1) * lr)
    e_ct = pltpu.make_async_remote_copy(
        src_ref=ct_h.at[others],
        dst_ref=ct_h.at[others],
        send_sem=ct_send.at[0],
        recv_sem=ct_recv.at[0],
        device_id={"col": other},
        device_id_type=MESH,
    )
    e_ct.wait_recv()
    own[1].wait()

    def signal(i0):
        z, r = norm(block(in_mixed, i0, lc))
        ct = ct_h[pl.ds(i0, lc)].reshape(lc * lc, c).astype(F32)
        put(ct32, i0, lc, ct)
        dz = rounded(dot_t(ct * block(in_gate, i0, lc), wo[1]))
        v = norm_back(z, r, dz).astype(BF16)
        put_half(sig, i0, lc, v.astype(F32))
        return v

    sig_out[...] = signal(o0).reshape(lc, lc, c)
    e_sig = pltpu.make_async_remote_copy(
        src_ref=sig_out,
        dst_ref=sig_got,
        send_sem=psend.at[2],
        recv_sem=precv.at[4],
        device_id={"col": other},
        device_id_type=MESH,
    )
    e_sig.start()
    e_in_right.wait_recv()

    def turn_signal(j0):
        for b in range(lc // TILE):
            t = jnp.swapaxes(sig[pl.ds(c0 + b * TILE, TILE), pl.ds(j0, lc), :], 0, 1)
            flip_s[:, b * TILE : (b + 1) * TILE, :] = t

    def left_row(j0, acc):
        return triangle(
            lr, lc, 0, lc,
            lambda a, q: in_right[r0 + a, pl.ds(j0 + q, 1), :],
            lambda q: flip_s[q],
            acc,
        )

    def left_col(j0, acc):
        return triangle(
            lr, n, 0, lc,
            lambda a, q: sig[r0 + a, pl.ds(j0 + q, 1), :],
            lambda q: right_t[j0 + q],
            acc,
        )

    def keep(ref, start, width, acc, fix=lambda v: v):
        for a in range(lr):
            ref[start + a * width : start + (a + 1) * width] = fix(acc[a])

    def kept(ref, start, width):
        return [ref[start + a * width : start + (a + 1) * width] for a in range(lr)]

    def window(late):
        def step(wide, m):
            signal(c0)
            z1, _ = norm(strips(in_mixed, wide))
            u1 = dot(z1, wo[1])
            if late:
                prepare(wide, m)
            elif wide:
                transposed(in_left, left_t, o0)
                transposed(in_right, right_t, o0)
            turn_signal(c0)
            keep(d_right, 0, lc, triangle(
                lr, lc, 0, n,
                lambda a, q: in_left[r0 + a, pl.ds(q, 1), :],
                lambda q: sig[q, pl.ds(c0, lc), :],
            ), rounded)
            keep(d_left, 0, lc, left_row(c0, None))
            if wide:
                if late:
                    for j0 in (c0, o0):
                        transposed(in_left, left_t, j0)
                        transposed(in_right, right_t, j0)
                keep(d_right, nr, n, triangle(
                    lr, n, 0, n,
                    lambda a, q: sig[q, pl.ds(r0 + a, 1), :],
                    lambda q: left_t[q],
                ), rounded)
                keep(d_left, nr, n, left_col(c0, None))
            saved[7, :m] = strips(ct32, wide) * u1

        return step

    each(window(False), my_col == 0)
    each(window(True), my_col == 1)
    e_sig.wait_recv()

    def back(wide, m):
        for b in range(lc // TILE):
            t = sig_got[b * TILE : (b + 1) * TILE].astype(F32)
            flip_s[:, b * TILE : (b + 1) * TILE, :] = jnp.swapaxes(t, 0, 1)
        keep(d_left, 0, lc, left_row(o0, kept(d_left, 0, lc)), rounded)
        if wide:
            sig[pl.ds(r0, lr), pl.ds(o0, lc), :] = sig_got[pl.ds(jl, lr)].astype(F32)
            keep(d_left, nr, n, left_col(o0, kept(d_left, nr, n)), rounded)
        f = tuple(saved[q, :m] for q in range(7))
        g = rounded(strips(ct32, wide) + front_back(f, wf[1], d_left[:m], d_right[:m], saved[7, :m]))
        z0, r = norm(strips(mixed, wide))
        dz = rounded(dot_t(g * strips(gate, wide), wo[0]))
        s = rounded(norm_back(z0, r, dz))
        along_row = s[:nr].reshape(lr, lc, c)
        sig_row[:, pl.ds(c0, lc), :] = along_row
        saved[8, :nr] = g[:nr]
        if wide:
            sig_col[...] = s[nr:].reshape(lr, n, c)

    each(back)
    e_row = partner(3, 5, sig_row.at[:, pl.ds(c0, lc)])
    e_row.start()
    e_col = partner(4, 6, sig_col)

    @pl.when(owner)
    def _():
        e_col.start()

    x = x_h[pl.ds(r0, lr)].reshape(nr, c).astype(F32)
    f = factors(x, row_of(mask), wf[0])
    z0, _ = norm(row_of(mixed))
    g = saved[8, :nr]
    d_gate = g * dot(z0, wo[0])

    def out_left(j0, acc):
        return triangle(
            lr, lc, 0, lc,
            lambda a, q: sig_row[a, pl.ds(j0 + q, 1), :],
            lambda q: right[j0 + q, pl.ds(c0, lc), :],
            acc,
        )

    acc = out_left(c0, None)
    e_row.wait_recv()
    d_a = jnp.concatenate([rounded(v) for v in out_left(o0, acc)], axis=0)

    @pl.when(jnp.logical_not(owner))
    def _():
        e_col.wait_recv()

    d_b = jnp.concatenate([rounded(v) for v in triangle(
        lr, lc, 0, n,
        lambda a, q: sig_col[a, pl.ds(q, 1), :],
        lambda q: left[q, pl.ds(c0, lc), :],
    )], axis=0)
    out[...] = (g + front_back(f, wf[0], d_a, d_b, d_gate)).astype(BF16).reshape(lr, lc, c)

    higher(drain)
    e_ct.wait_send()
    pair_bytes(0, lambda copy: copy.wait_send())

    @pl.when(wide_row)
    def _():
        far_copy().wait_send()

    for copy in (partner(1, 3, in_left), e_sig, e_row):
        copy.wait_send()

    @pl.when(owner)
    def _():
        e_col.wait_send()


def from_root(array, axis, root):
    mine = lax.axis_index(axis) == root
    return lax.psum(jnp.where(mine, array, jnp.zeros_like(array)), axis)


def layer_norm(values):
    centred = values - jnp.mean(values, axis=-1, keepdims=True)
    spread = jnp.mean(centred * centred, axis=-1, keepdims=True)
    return centred * lax.rsqrt(spread + 1e-05)


def project_pair(inner_pair, mask_pair, weight):
    normed = layer_norm(inner_pair.astype(jnp.float32)).astype(jnp.bfloat16)
    linear = jnp.dot(normed, weight, preferred_element_type=jnp.float32)
    left_side = jax.nn.sigmoid(linear[..., :H]) * linear[..., H : 2 * H]
    right_side = jax.nn.sigmoid(linear[..., 2 * H : 3 * H]) * linear[..., 3 * H : 4 * H]
    operands = (jnp.stack((left_side, right_side)) * mask_pair[None, :, :, None]).astype(
        jnp.bfloat16
    )
    return (operands, jax.nn.sigmoid(linear[..., 4 * H :]))


def finish(mixed_part, gate_value, inner_pair, weight):
    normed = layer_norm(mixed_part).astype(jnp.bfloat16)
    update = jnp.dot(normed, weight, preferred_element_type=jnp.float32)
    return (inner_pair.astype(jnp.float32) + gate_value * update).astype(jnp.bfloat16)


def body(pair_act, cotangent, residue_mask, front_weight, out_weight):
    local_rows = pair_act.shape[0]
    local_cols = pair_act.shape[1]
    row_index = lax.axis_index("row")
    col_index = lax.axis_index("col")
    block_rows = lax.axis_size("row") // lax.axis_size("col")
    owner_col = row_index // block_rows
    offset = row_index % block_rows * local_rows
    chain_mask = residue_mask.astype(jnp.float32)
    mask_rows = lax.dynamic_slice_in_dim(chain_mask, row_index * local_rows, local_rows)
    mask_cols = lax.dynamic_slice_in_dim(chain_mask, col_index * local_cols, local_cols)
    mask_pair = mask_rows[:, None] * mask_cols[None, :]

    def gather_rows(stacked):
        return lax.all_gather(stacked, "row", axis=1, tiled=True)

    def column_block(gathered):
        slab = lax.dynamic_slice_in_dim(gathered, offset, local_rows, 1)
        return from_root(slab, "col", owner_col)

    def gather_cols(values):
        return lax.all_gather(values, "col", axis=1, tiled=True)

    def sum_cols(partial_term):
        return lax.psum_scatter(
            partial_term.astype(jnp.bfloat16), "col", scatter_dimension=1, tiled=True
        ).astype(jnp.float32)

    (out_ops, out_gate), out_front_back = jax.vjp(
        lambda inner_pair: project_pair(inner_pair, mask_pair, front_weight[0]), pair_act
    )
    fetched = gather_rows(out_ops)
    out_mixed = sum_cols(
        jnp.einsum("ikc,jkc->ijc", out_ops[0], fetched[-1], preferred_element_type=jnp.float32)
    )
    pair_mid, out_finish_back = jax.vjp(
        lambda mixed_part, gate_value, inner_pair: finish(
            mixed_part, gate_value, inner_pair, out_weight[0]
        ),
        out_mixed,
        out_gate,
        pair_act,
    )
    (in_ops, in_gate), in_front_back = jax.vjp(
        lambda inner_pair: project_pair(inner_pair, mask_pair, front_weight[1]), pair_mid
    )
    in_fetched = gather_rows(in_ops)
    left_block = column_block(in_fetched[0])
    in_mixed = jnp.einsum(
        "kic,kjc->ijc", left_block, in_fetched[1], preferred_element_type=jnp.float32
    )
    unused_pair, in_finish_back = jax.vjp(
        lambda mixed_part, gate_value, inner_pair: finish(
            mixed_part, gate_value, inner_pair, out_weight[1]
        ),
        in_mixed,
        in_gate,
        pair_mid,
    )
    grad_mixed, grad_gate, grad_inner = in_finish_back(cotangent)
    signal = grad_mixed.astype(jnp.bfloat16)
    signal_rows = gather_rows(signal[None])[0]
    left_rows = gather_cols(in_ops[0])
    grad_right = jnp.einsum(
        "kic,ijc->kjc", left_rows, signal_rows, preferred_element_type=jnp.float32
    )
    grad_left = sum_cols(
        jnp.einsum("kjc,ijc->kic", in_ops[1], signal_rows, preferred_element_type=jnp.float32)
    )
    (grad_front,) = in_front_back(
        (jnp.stack((grad_left, grad_right)).astype(jnp.bfloat16), grad_gate)
    )
    grad_mid = (grad_inner.astype(jnp.float32) + grad_front.astype(jnp.float32)).astype(
        jnp.bfloat16
    )
    grad_mixed, grad_gate, grad_inner = out_finish_back(grad_mid)
    signal = grad_mixed.astype(jnp.bfloat16)
    signal_cols = gather_cols(signal)
    grad_left = jnp.einsum(
        "ijc,jkc->ikc", signal_cols, fetched[-1], preferred_element_type=jnp.float32
    )
    signal_block = column_block(gather_rows(signal[None])[0])
    grad_right = jnp.einsum(
        "ijc,ikc->jkc", signal_block, fetched[0], preferred_element_type=jnp.float32
    )
    (grad_front,) = out_front_back(
        (jnp.stack((grad_left, grad_right)).astype(jnp.bfloat16), grad_gate)
    )
    return (grad_inner.astype(jnp.float32) + grad_front.astype(jnp.float32)).astype(jnp.bfloat16)


def crop_body(rows, pair_act, cotangent, residue_mask, front_weight, out_weight):
    lr, lc, c = pair_act.shape
    n = residue_mask.shape[0]
    strip = lr * lc + lr * n
    dma = pltpu.SemaphoreType.DMA
    operands = (pair_act, cotangent, residue_mask.reshape(1, n), front_weight, out_weight)
    return pl.pallas_call(
        functools.partial(crop_kernel, rows),
        out_shape=jax.ShapeDtypeStruct((lr, lc, c), BF16),
        in_specs=[pl.BlockSpec(memory_space=pl.ANY)] * 5,
        out_specs=pl.BlockSpec(memory_space=pltpu.VMEM),
        scratch_shapes=[
            pltpu.VMEM((n, lc, c), BF16),
            pltpu.VMEM((n, lc, c), BF16),
            pltpu.VMEM((2 * lr, lc, c), BF16),
            pltpu.VMEM(front_weight.shape, BF16),
            pltpu.VMEM(out_weight.shape, BF16),
            pltpu.VMEM((1, n), jnp.int32),
        ]
        + [pltpu.VMEM((n, n, c), F32)] * 7
        + [pltpu.VMEM((lc, lc, c), F32)] * 2
        + [pltpu.VMEM((n * lc, c), F32)] * 7
        + [
            pltpu.VMEM((n * lc, c), BF16),
            pltpu.VMEM((n, c), F32),
            pltpu.VMEM((9, strip, c), F32),
            pltpu.VMEM((strip, c), F32),
            pltpu.VMEM((strip, c), F32),
            pltpu.VMEM((lr, n, c), F32),
            pltpu.VMEM((lr, n, c), F32),
            pltpu.VMEM((lc, lc, c), BF16),
            pltpu.VMEM((lc, lc, c), BF16),
        ]
        + [dma((5,)), dma((rows,)), dma((rows,)), dma((1,)), dma((1,)), dma((5,)), dma((7,))]
        + [pltpu.SemaphoreType.REGULAR((rows + 1,)), dma((1,)), dma((2,))],
        compiler_params=pltpu.CompilerParams(
            collective_id=0, has_side_effects=True, vmem_limit_bytes=VMEM_BUDGET
        ),
    )(*[pltpu.with_memory_space_constraint(v, pltpu.HBM) for v in operands])


def fits(mesh, n, lr, lc, c):
    rows, cols = mesh.shape["row"], mesh.shape["col"]
    return (
        cols == 2
        and rows >= 2
        and rows & (rows - 1) == 0
        and n == 2 * lc
        and lc == 2 * TILE
        and lc % (2 * lr) == 0
        and FULL_ARRAYS * 4 * n * n * c <= VMEM_BUDGET
    )


def solution(mesh):
    def dispatch(pair_act, cotangent, residue_mask, front_weight, out_weight):
        n = residue_mask.shape[0]
        if fits(mesh, n, *pair_act.shape):
            return crop_body(
                mesh.shape["row"], pair_act, cotangent, residue_mask, front_weight, out_weight
            )
        return body(pair_act, cotangent, residue_mask, front_weight, out_weight)

    placed = (P(("grp", "row"), "col", None), P(("grp", "row"), "col", None), P("grp"), P(), P())
    return jax.shard_map(
        dispatch,
        mesh=mesh,
        in_specs=placed,
        out_specs=P(("grp", "row"), "col", None),
        check_vma=False,
    )
```

profile of v0, /device:TPU:0, one launch (start us, length us, event | category | flops | bytes accessed | tf_op | source)
XLA Modules:
  0.0 16.0 jit_solution(10560103400071428714)
XLA Ops:
  0.0 15.4 %shard_map.55 = bf16[4,16,128]{2,1,0:T(8,128)(2,1)S(1)} custom-call(bf16[4,16,128]{2,1,0:T(8,128)(2,1)} %pair.1, bf16[4,16,128]{2,1,0:T(8,128)(2,1)} %cot.1, s32[1,32]{1,0:T(1,128)} %bitcast.1, bf16[2,128,640]{2,1,0:T(8,128)(2,1)} %wf_in.1, bf16[2,128,128]{2,1,0:T(8,128)(2,1)} %wo_in.1), custom_call_target="tpu_custom_call" | custom-call | tf_op jit(solution)/shard_map/pallas_call | solution.py:774
  15.4 0.6 %copy.7 = bf16[4,16,128]{2,1,0:T(8,128)(2,1)} copy(bf16[4,16,128]{2,1,0:T(8,128)(2,1)S(1)} %shard_map.55) | data formatting | bytes 32768
where the time goes:
time: 16.4 us; the launch traced here: 16 us
  Pallas kernels  15.4 us (94%)
  local copies, waits for them, and re-layouts  0.61 us (4%)
    pallas_call x1, Pallas kernels, crop_body(): pl.pallas_call(functools.partial(crop_kernel, rows), out_shape=jax.ShapeD...  15.4 us
    unnamed x1, local copies, waits for them, and re-layouts  0.61 us

commit v1 on v0

--- a/solution.py
+++ b/solution.py
@@ -132,6 +132,14 @@
     for copy in [chain_copy, own[0]] + weights + [own[1]]:
         copy.start()
 
+    def group_of(row):
+        if not isinstance(row, int):
+            return 0
+        apart = 0
+        for b in range(1, bits):
+            apart = apart + (1 - me_bits[b] if row >> b & 1 else me_bits[b]) * (1 << b)
+        return jnp.maximum(lax.div(apart, 2) - 1, 0)
+
     def direct(t, row, mine=None):
         src, dst = ((pair, x_h), (cot, ct_h))[t]
         source = row if mine is None else mine
@@ -139,7 +147,7 @@
             src_ref=src,
             dst_ref=dst.at[pl.ds(pl.multiple_of(source * lr, lr), lr)],
             send_sem=x_send.at[row] if t == 0 else ct_send.at[0],
-            recv_sem=x_recv.at[source] if t == 0 else ct_recv.at[0],
+            recv_sem=x_recv.at[group_of(row)] if t == 0 else ct_recv.at[0],
             device_id={"row": row},
             device_id_type=MESH,
         )
@@ -282,12 +290,18 @@
     groups = [[(0, 1)], [(1, 1), (2, 2)] if rows > 2 else [(1, 1)]]
     groups += [[(d, 2)] for d in range(4, rows, 2)]
     for g, group in enumerate(groups):
-        for d, count in group:
-            for q in range(d, d + count):
-                if q == 0:
-                    own[0].wait()
-                else:
-                    direct(0, flip(q)).wait_recv()
+        if g == 0:
+            own[0].wait()
+        else:
+            here = x_h.at[pl.ds(0, sum(count for _, count in group) * lr)]
+            pltpu.make_async_remote_copy(
+                src_ref=here,
+                dst_ref=here,
+                send_sem=x_send.at[0],
+                recv_sem=x_recv.at[g - 1],
+                device_id={"col": other},
+                device_id_type=MESH,
+            ).wait_recv()
         segments = [
             (pl.multiple_of(flip(d, count.bit_length() - 1) * lr, count * lr), count * lr)
             for d, count in group
@@ -798,7 +812,7 @@
             pltpu.VMEM((lc, lc, c), BF16),
             pltpu.VMEM((lc, lc, c), BF16),
         ]
-        + [dma((5,)), dma((rows,)), dma((rows,)), dma((1,)), dma((1,)), dma((5,)), dma((7,))]
+        + [dma((5,)), dma((rows,)), dma((max(rows // 2 - 1, 1),)), dma((1,)), dma((1,)), dma((5,)), dma((7,))]
         + [pltpu.SemaphoreType.REGULAR((rows + 1,)), dma((1,)), dma((2,))],
         compiler_params=pltpu.CompilerParams(
             collective_id=0, has_side_effects=True, vmem_limit_bytes=VMEM_BUDGET

time: 16.4 us -> 16.3 us (level)
  the two profiles are of different devices: /device:TPU:0 before, /device:TPU:24 now
where the time goes in v1:
time: 16.3 us; the launch traced here: 16.2 us
  Pallas kernels  15.5 us (95%)
  local copies, waits for them, and re-layouts  0.61 us (4%)
    pallas_call x1, Pallas kernels, crop_body(): pl.pallas_call(functools.partial(crop_kernel, rows), out_shape=jax.ShapeD...  15.5 us
    unnamed x1, local copies, waits for them, and re-layouts  0.61 us

profile of v1, /device:TPU:24, one launch (start us, length us, event | category | flops | bytes accessed | tf_op | source)
XLA Modules:
  0.0 16.2 jit_solution(150487822710582174)
XLA Ops:
  0.0 15.5 %shard_map.55 = bf16[4,16,128]{2,1,0:T(8,128)(2,1)S(1)} custom-call(bf16[4,16,128]{2,1,0:T(8,128)(2,1)} %pair.1, bf16[4,16,128]{2,1,0:T(8,128)(2,1)} %cot.1, s32[1,32]{1,0:T(1,128)} %bitcast.1, bf16[2,128,640]{2,1,0:T(8,128)(2,1)} %wf_in.1, bf16[2,128,128]{2,1,0:T(8,128)(2,1)} %wo_in.1), custom_call_target="tpu_custom_call" | custom-call | tf_op jit(solution)/shard_map/pallas_call | solution.py:788
  15.6 0.6 %copy.7 = bf16[4,16,128]{2,1,0:T(8,128)(2,1)} copy(bf16[4,16,128]{2,1,0:T(8,128)(2,1)S(1)} %shard_map.55) | data formatting | bytes 32768

commit v2 on v1

--- a/solution.py
+++ b/solution.py
@@ -418,8 +418,9 @@
     normed[...] = x
     p = dot(x, wf[1, :, : 2 * H])
     put_half(in_left, 0, n, rounded(sigmoid(scaled(p, 0, 0)) * scaled(p, 1, 0) * mask[...]))
+    quarter = n // 4
     e_in_left = [
-        partner(1, 1 + b, in_left.at[:, pl.ds(c0 + b * TILE, TILE)]) for b in range(lc // TILE)
+        partner(1, r, half(in_left, b * quarter, quarter)) for b, r in enumerate((1, 2, 7, 8))
     ]
     for copy in e_in_left:
         copy.start()
@@ -430,23 +431,25 @@
     e_in_right = partner(1, 3, half(in_right, 0, n))
     e_in_right.start()
 
-    def incoming(i0, copies=()):
-        few = 4
-
-        def step(i1):
-            acc = triangle(
-                few, lc, 0, n,
-                lambda a, q: in_left[q, pl.ds(i1 + a, 1), :],
-                lambda q: in_right[q, pl.ds(c0, lc), :],
-            )
-            for a in range(few):
-                in_mixed[pl.ds(pl.multiple_of((i1 + a) * lc, lc), lc), :] = acc[a]
-
-        for b in range(lc // TILE):
-            if copies:
-                copies[b].wait_recv()
-            for a in range(0, TILE, few):
-                step(pl.multiple_of(i0 + b * TILE, TILE) + a)
+    def incoming(i0, copies=(None,)):
+        depth = n // len(copies)
+        for q, copy in enumerate(copies):
+            if copy is not None:
+                copy.wait_recv()
+            for b in range(lc // TILE):
+                i1 = pl.multiple_of(i0 + b * TILE, TILE)
+                at = pl.multiple_of(i1 * lc, lc)
+                acc = None
+                if q:
+                    acc = [in_mixed[pl.ds(at + a * lc, lc), :] for a in range(TILE)]
+                acc = triangle(
+                    TILE, lc, q * depth, depth,
+                    lambda a, k: in_left[k, pl.ds(i1 + a, 1), :],
+                    lambda k: in_right[k, pl.ds(c0, lc), :],
+                    acc,
+                )
+                for a in range(TILE):
+                    in_mixed[pl.ds(at + a * lc, lc), :] = acc[a]
 
     nr, nc = lr * lc, lr * n
 
@@ -812,7 +815,7 @@
             pltpu.VMEM((lc, lc, c), BF16),
             pltpu.VMEM((lc, lc, c), BF16),
         ]
-        + [dma((5,)), dma((rows,)), dma((max(rows // 2 - 1, 1),)), dma((1,)), dma((1,)), dma((5,)), dma((7,))]
+        + [dma((5,)), dma((rows,)), dma((max(rows // 2 - 1, 1),)), dma((1,)), dma((1,)), dma((5,)), dma((9,))]
         + [pltpu.SemaphoreType.REGULAR((rows + 1,)), dma((1,)), dma((2,))],
         compiler_params=pltpu.CompilerParams(
             collective_id=0, has_side_effects=True, vmem_limit_bytes=VMEM_BUDGET

time: 16.3 us -> 16.2 us (level)
  the two profiles are of different devices: /device:TPU:24 before, /device:TPU:20 now
where the time goes in v2:
time: 16.2 us; the launch traced here: 16.1 us
  Pallas kernels  15.5 us (96%)
  local copies, waits for them, and re-layouts  0.61 us (4%)
    pallas_call x1, Pallas kernels, crop_body(): pl.pallas_call(functools.partial(crop_kernel, rows), out_shape=jax.ShapeD...  15.5 us
    unnamed x1, local copies, waits for them, and re-layouts  0.61 us

profile of v2, /device:TPU:20, one launch (start us, length us, event | category | flops | bytes accessed | tf_op | source)
XLA Modules:
  0.0 16.1 jit_solution(5840498577932441266)
XLA Ops:
  0.0 15.5 %shard_map.55 = bf16[4,16,128]{2,1,0:T(8,128)(2,1)S(1)} custom-call(bf16[4,16,128]{2,1,0:T(8,128)(2,1)} %pair.1, bf16[4,16,128]{2,1,0:T(8,128)(2,1)} %cot.1, s32[1,32]{1,0:T(1,128)} %bitcast.1, bf16[2,128,640]{2,1,0:T(8,128)(2,1)} %wf_in.1, bf16[2,128,128]{2,1,0:T(8,128)(2,1)} %wo_in.1), custom_call_target="tpu_custom_call" | custom-call | tf_op jit(solution)/shard_map/pallas_call | solution.py:791
  15.5 0.6 %copy.7 = bf16[4,16,128]{2,1,0:T(8,128)(2,1)} copy(bf16[4,16,128]{2,1,0:T(8,128)(2,1)S(1)} %shard_map.55) | data formatting | bytes 32768
